TPU v7x, 256 devices: a whole 4x4x8 slice. The times are simulated.
256 devices in a mesh: ep: 32 (over x, z), tp: 8 (over y, core).
Axes of the slice: x: 4, y: 4, z: 8, core: 2. Of those that a mesh axis runs over, the one named last changes fastest.
Arguments:
- attn_out: bfloat16 [8192, 2048], P('ep', 'tp'), may hold values from -6 to 6
- out_proj: bfloat16 [2048, 2048], P('tp'), may hold values from -0.125 to 0.125
- residual: bfloat16 [8192, 2048], P('ep'), may hold values from -40 to 40
- norm_gain: float32 [2048], replicated, may hold values from 0.25 to 1.75
- router: bfloat16 [2048, 64], replicated, may hold values from -0.125 to 0.125
- expert_gate_up: bfloat16 [256, 2, 352, 2048], P(('ep', 'tp')), may hold values from -0.125 to 0.125
- expert_down: bfloat16 [256, 352, 2048], P(('ep', 'tp')), may hold values from -0.15625 to 0.15625
- shared_gate_up: bfloat16 [2, 2816, 2048], P(None, 'tp'), may hold values from -0.125 to 0.125
- shared_down: bfloat16 [2816, 2048], P('tp'), may hold values from -0.109375 to 0.109375
- routes: int32 [8192, 6], P('ep'), may hold values from 0 to 63, all different within a row; in each aligned block of 256 rows (0 to 255, 256 to 511, ...) at most 40 rows name the same one
- live_rows: int32 [32], P('ep'), may hold values from 128 to 256, as said below
- next_gain: float32 [2048], replicated, may hold values from 0.25 to 1.75
Outputs:
- next_stream: bfloat16 [8192, 2048], P('ep', 'tp')
- next_normed: bfloat16 [8192, 2048], P('ep', 'tp')
Inputs may be any that keep to these rules, and one draw needn't show every extreme that they name: `routes`: each row names 6 different experts. Among the 256 rows of one block no expert is named by more than 40 rows, a bound that some block reaches. The live rows of block b are its first live_rows[b] rows; in every draw some block is entirely live.
All inputs are finite; a program needn't handle non-finite values.
Results may differ from a plain program's by a relative error of at most 0.012.
Values may be sent and summed in bfloat16 or wider, within the bound.
A program may use at most 128 MiB of HBM per device.

v0:
```python
import jax
import jax.numpy as jnp
from jax import lax
from jax.sharding import PartitionSpec as P

EXP_DEV = 2
norm_epsilon = 1e-06
routed_scale = 2.446


def slot_table(route_block, live_count, experts, capacity):
    fanout = route_block.shape[1]
    flat_ids = route_block.reshape(-1)
    entry_index = jnp.arange(flat_ids.shape[0], dtype=jnp.int32)
    living = entry_index // fanout < live_count
    one_hot = (
        (flat_ids[:, None] == jnp.arange(experts, dtype=jnp.int32)[None, :]) & living[:, None]
    ).astype(jnp.int32)
    earlier = jnp.cumsum(one_hot, axis=0, dtype=jnp.int32) - one_hot
    position = jnp.sum(earlier * one_hot, axis=1, dtype=jnp.int32)
    slot_index = jnp.where(living, flat_ids * capacity + position, experts * capacity)
    slot_owner = (
        jnp.full((experts * capacity,), -1, jnp.int32).at[slot_index].set(entry_index, mode="drop")
    )
    return (slot_index, living, slot_owner)


def gate_weights(normed, router, route_block):
    logits = jnp.dot(normed, router, preferred_element_type=jnp.float32)
    chosen = jnp.take_along_axis(logits, route_block, axis=1)
    scores = jax.nn.sigmoid(chosen)
    return scores / jnp.sum(scores, axis=1, keepdims=True) * routed_scale


def on_device(
    attn_out,
    out_proj,
    residual,
    norm_gain,
    router,
    expert_gate_up,
    expert_down,
    shared_gate_up,
    shared_down,
    routes,
    live_rows,
    next_gain,
):
    partial_out = jnp.dot(attn_out, out_proj, preferred_element_type=jnp.float32)
    summed = lax.psum(partial_out, "tp")
    stream = (summed + residual.astype(jnp.float32)).astype(jnp.bfloat16)
    stream_wide = stream.astype(jnp.float32)
    normed = (
        stream_wide
        * lax.rsqrt(jnp.mean(stream_wide * stream_wide, axis=1, keepdims=True) + norm_epsilon)
        * norm_gain
    ).astype(jnp.bfloat16)
    width = normed.shape[1]
    tp_count = lax.axis_size("tp")
    ep_count = lax.axis_size("ep")
    width_slice = width // tp_count
    column_start = lax.axis_index("tp") * width_slice
    unit_blocks = tp_count // EXP_DEV
    group = lax.axis_index("tp") // unit_blocks
    experts = router.shape[1]
    fanout = routes.shape[1]
    token_rows = routes.shape[0]
    capacity = token_rows * fanout * 5 // (3 * experts)
    slot_index, living, slot_owner = slot_table(routes, live_rows[0], experts, capacity)
    owners = slot_owner.reshape(ep_count, EXP_DEV, capacity)
    filled = owners >= 0
    source_row = jnp.where(filled, owners // fanout, 0)
    dispatched = jnp.where(filled[:, :, :, None], normed[source_row], jnp.zeros((), jnp.bfloat16))
    rows = lax.dynamic_index_in_dim(
        lax.all_to_all(dispatched, "ep", split_axis=0, concat_axis=0, tiled=True),
        group,
        1,
        keepdims=False,
    )
    gate_proj = jnp.einsum(
        "scd,fd->scf", rows, expert_gate_up[0, 0], preferred_element_type=jnp.float32
    )
    up_proj = jnp.einsum(
        "scd,fd->scf", rows, expert_gate_up[0, 1], preferred_element_type=jnp.float32
    )
    hidden = (jax.nn.silu(gate_proj) * up_proj).astype(jnp.bfloat16)
    produced = jnp.einsum(
        "scf,fd->scd", hidden, expert_down[0], preferred_element_type=jnp.float32
    ).astype(jnp.bfloat16)
    returned = lax.all_to_all(produced, "ep", split_axis=0, concat_axis=0, tiled=True)
    flat_terms = returned.reshape(ep_count * capacity, width)
    living_pairs = living.reshape(token_rows, fanout)
    mine = living_pairs & (routes % EXP_DEV == group)
    position = slot_index.reshape(token_rows, fanout) - routes * capacity
    term_row = jnp.where(mine, routes // EXP_DEV * capacity + position, 0)
    weights = gate_weights(normed, router, routes) * mine.astype(jnp.float32)
    picked = flat_terms[term_row]
    routed_part = jnp.einsum("tkd,tk->td", picked.astype(jnp.float32), weights)
    shared_gate = jnp.einsum(
        "td,fd->tf", normed, shared_gate_up[0], preferred_element_type=jnp.float32
    )
    shared_up = jnp.einsum(
        "td,fd->tf", normed, shared_gate_up[1], preferred_element_type=jnp.float32
    )
    shared_hidden = (jax.nn.silu(shared_gate) * shared_up).astype(jnp.bfloat16)
    shared_part = jnp.dot(shared_hidden, shared_down, preferred_element_type=jnp.float32)
    combined = lax.psum_scatter(
        (routed_part + shared_part).astype(jnp.bfloat16), "tp", scatter_dimension=1, tiled=True
    ).astype(jnp.float32)
    stream_slice = lax.dynamic_slice_in_dim(stream, column_start, width_slice, 1)
    next_stream = (stream_slice.astype(jnp.float32) + combined).astype(jnp.bfloat16)
    next_wide = next_stream.astype(jnp.float32)
    squares = lax.psum(jnp.sum(next_wide * next_wide, axis=1), "tp")
    gain_slice = lax.dynamic_slice_in_dim(next_gain, column_start, width_slice, 0)
    next_normed = (
        next_wide * lax.rsqrt(squares[:, None] / width + norm_epsilon) * gain_slice
    ).astype(jnp.bfloat16)
    return (next_stream, next_normed)


def solution(mesh):
    in_specs = (
        P("ep", "tp"),
        P("tp", None),
        P("ep", None),
        P(),
        P(),
        P(("ep", "tp"), None, None, None),
        P(("ep", "tp"), None, None),
        P(None, "tp", None),
        P("tp", None),
        P("ep", None),
        P("ep"),
        P(),
    )
    out_specs = (P("ep", "tp"), P("ep", "tp"))
    return jax.shard_map(
        on_device, mesh=mesh, in_specs=in_specs, out_specs=out_specs, check_vma=False
    )
```

profile of v0, /device:TPU:1, one launch (start us, length us, event | category | flops | bytes accessed | tf_op | source)
XLA Modules:
  0.0 608.2 jit_solution(8504731297024068242)
XLA Ops:
  7.2 0.0 copy-start
  7.2 0.0 copy-start.4
  7.2 0.0 all-reduce.2.cloned.1.call-start
  7.2 3.1 fusion.76
  10.4 0.0 all-reduce.2.cloned.1.call-update
  10.4 0.0 copy-done.4
  10.4 0.1 copy.42
  10.5 0.1 eq.37
  10.7 0.1 eq.33
  11.5 0.1 fusion.37
  11.6 18.1 %reduce-window.6 = s32[64,12,128]{2,1,0:T(8,128)S(1)} reduce-window(s32[64,12,128]{2,1,0:T(8,128)S(1)} %fusion.37, s32[]{:T(128)} %constant.103.clone.1), window={size=1x1x128 pad=0_0x0_0x127_0}, to_apply=%region_1.0 | reduce-window | flops 12484608 | bytes 786436 | tf_op jit(solution)/shard_map/reduce-window
  29.7 0.2 slice.30
  29.9 0.3 copy.44
  30.2 0.1 copy.45
  30.3 0.2 broadcast_add_fusion
  30.5 0.2 fusion.40
  30.7 0.1 reduce_sum.43
  30.9 0.1 copy.46
  31.0 0.1 copy.41
  31.1 0.1 mul.91
  31.3 6.2 %scatter_custom_fusion = s32[2560]{0:T(1024)S(1)} fusion(s32[1536]{0:T(1024)S(1)} %fusion.67, s32[1536]{0:T(1024)S(1)} %iota.72, s32[]{:T(128)} %constant.107.clone.1), kind=kCustom, calls=%fused_computation.112 | custom fusion | bytes 10244 | tf_op jit(solution)/shard_map/scatter | solution.py:23
  37.5 0.1 ge.28
  37.7 0.7 ge.27
  38.4 0.1 div.89
  38.5 0.1 and.83
  38.6 0.1 compare_select_fusion
  38.7 0.1 reshape.223
  38.8 0.6 pad_clamp_fusion
  39.4 44.1 %all-reduce.2.cloned.1.call-done = f32[256,2048]{1,0:T(8,128)} async-done(((f32[256,2048]{1,0:T(8,128)}), f32[256,2048]{1,0:T(8,128)}) %all-reduce.2.cloned.1.call-update) | async-done | bytes 2097168 | tf_op jit(solution)/shard_map/psum | solution.py:50
  83.4 2.3 fusion.7
  85.7 0.0 copy-done.5
  85.7 0.3 fusion.9
  86.0 10.9 %gather_fusion = bf16[2560,2048]{1,0:T(8,128)(2,1)} fusion(bf16[256,2048]{1,0:T(8,128)(2,1)S(1)} %fusion.9, s32[3072]{0:T(1024)} %pad_clamp_fusion), kind=kCustom, calls=%fused_computation | custom fusion | bytes 20981760 | tf_op jit(solution)/shard_map/gather | solution.py:73
  97.0 10.0 %broadcast_select_fusion = bf16[32,2,40,2048]{3,2,1,0:T(8,128)(2,1)} fusion(bf16[32,2,40,2048]{3,2,1,0:T(8,128)(2,1)} %bitcast.83, pred[32,2,40]{2,1,0:T(4,128)(4,1)} %ge.27), kind=kLoop, calls=%fused_computation.4 | loop fusion | flops 5242880 | bytes 20974080 | tf_op jit(solution)/shard_map/jit(_where)/select_n | solution.py:73
  106.9 9.7 %all-to-all-start = ((bf16[32,2,40,2048]{3,2,1,0:T(8,128)(2,1)}), bf16[32,2,40,2048]{3,2,1,0:T(8,128)(2,1)}, u32[]{:S(2)}, u32[]{:S(2)}) async-start(bf16[32,2,40,2048]{3,2,1,0:T(8,128)(2,1)} %broadcast_select_fusion), calls=%async_computation | async-start | bytes 20971520 | tf_op jit(solution)/shard_map/all_to_all | solution.py:75
  116.6 232.0 %all-to-all-done = bf16[32,2,40,2048]{3,2,1,0:T(8,128)(2,1)} async-done(((bf16[32,2,40,2048]{3,2,1,0:T(8,128)(2,1)}), bf16[32,2,40,2048]{3,2,1,0:T(8,128)(2,1)}, u32[]{:S(2)}, u32[]{:S(2)}) %all-to-all-start) | async-done | bytes 10485792 | tf_op jit(solution)/shard_map/all_to_all | solution.py:75
  348.6 7.1 %fusion.2 = f32[32,40,352]{2,1,0:T(8,128)} fusion(bf16[32,2,40,2048]{3,2,1,0:T(8,128)(2,1)} %all-to-all-done, s32[]{:T(128)S(6)} %select_n.135, bf16[1,2,352,2048]{3,2,1,0:T(8,128)(2,1)} %param.17), kind=kOutput, calls=%fused_computation.7 | convolution fusion | flops 1845493760 | bytes 8486916 | tf_op jit(solution)/shard_map/scd,fd->scf/dot_general | solution.py:80
  355.7 0.0 copy-done
  355.7 9.8 %convolution_convert_fusion = bf16[32,40,2048]{2,1,0:T(8,128)(2,1)} fusion(bf16[1,352,2048]{2,1,0:T(8,128)(2,1)S(1)} %copy-done, f32[32,40,352]{2,1,0:T(8,128)} %fusion.2, bf16[32,2,40,2048]{3,2,1,0:T(8,128)(2,1)} %all-to-all-done, s32[]{:T(128)S(6)} %select_n.135, bf16[1,2,352,2048]{3,2,1,0:T(8,128)(2,1)} %param.17), kind=kOutput, calls=%fused_computation.11 | convolution fusion | flops 3696312320 | bytes 15335428 | tf_op jit(solution)/shard_map/scf,fd->scd/dot_general | solution.py:87
  365.5 10.2 %all-to-all-start.1 = ((bf16[32,40,2048]{2,1,0:T(8,128)(2,1)}), bf16[32,40,2048]{2,1,0:T(8,128)(2,1)}, u32[]{:S(2)}, u32[]{:S(2)}) async-start(bf16[32,40,2048]{2,1,0:T(8,128)(2,1)} %convolution_convert_fusion), calls=%async_computation.1 | async-start | bytes 10485760 | tf_op jit(solution)/shard_map/all_to_all | solution.py:90
  375.7 0.2 reduce-scatter.2.cloned.1.call-start
  375.9 0.1 copy.47
  376.1 0.1 reshape.231
  376.2 0.1 copy.48
  376.4 0.1 reshape.237
  376.6 0.0 copy-done.3
  376.6 0.4 fusion.77
  377.0 12.7 %gather_fusion.2 = f32[1536]{0:T(1024)S(1)} fusion(f32[256,64]{0,1:T(8,128)S(1)} %fusion.77, s32[1536]{0:T(1024)S(1)} %reshape.237), kind=kCustom, calls=%fused_computation.2 | custom fusion | bytes 24576 | tf_op jit(solution)/shard_map/jit(take_along_axis)/gather | solution.py:30
  389.7 0.1 reshape.240
  389.9 0.1 copy.49
  390.0 0.2 copy.50
  390.2 2.7 fusion.16
  392.9 99.9 %all-to-all-done.1 = bf16[32,40,2048]{2,1,0:T(8,128)(2,1)} async-done(((bf16[32,40,2048]{2,1,0:T(8,128)(2,1)}), bf16[32,40,2048]{2,1,0:T(8,128)(2,1)}, u32[]{:S(2)}, u32[]{:S(2)}) %all-to-all-start.1) | async-done | bytes 5242912 | tf_op jit(solution)/shard_map/all_to_all | solution.py:90
  492.8 15.8 %gather_fusion.1 = bf16[1536,2048]{1,0:T(8,128)(2,1)} fusion(bf16[1280,2048]{1,0:T(8,128)(2,1)} %bitcast.11, s32[2048]{0:T(1024)S(1)} %pad_clamp_fusion.1), kind=kCustom, calls=%fused_computation.1 | custom fusion | bytes 12589056 | tf_op jit(solution)/shard_map/gather | solution.py:97
  508.7 10.9 %reshape.230 = bf16[256,6,2048]{2,1,0:T(8,128)(2,1)} reshape(bf16[1536,2048]{1,0:T(8,128)(2,1)} %gather_fusion.1) | data formatting | bytes 12582912 | tf_op jit(solution)/shard_map/gather | solution.py:97
  519.6 7.1 %fusion.78 = f32[256,1,2048]{2,1,0:T(1,128)} fusion(bf16[256,6,2048]{2,1,0:T(8,128)(2,1)} %reshape.230, bf16[256,6,1]{1,2,0:T(2,128)(2,1)S(1)} %copy.50), kind=kOutput, calls=%fused_computation.124 | convolution fusion | flops 6291456 | bytes 8391680 | tf_op jit(solution)/shard_map/tkd,tk->td/dot_general | solution.py:98
  526.7 5.9 fusion.6
  532.6 0.0 reduce-scatter.2.cloned.1.call-update
  532.6 0.8 dynamic_slice.12
  533.4 51.3 %reduce-scatter.2.cloned.1.call-done = bf16[256,256]{1,0:T(8,128)(2,1)} async-done(((bf16[256,2048]{1,0:T(8,128)(2,1)}), bf16[256,256]{1,0:T(8,128)(2,1)}) %reduce-scatter.2.cloned.1.call-update) | async-done | bytes 131088 | tf_op jit(solution)/shard_map/reduce_scatter | solution.py:107
  584.7 1.0 fusion.47
  585.7 0.0 copy-start.2
  585.7 14.9 %psum.15 = f32[256]{0:T(256)S(1)} all-reduce(f32[256]{0:T(256)S(1)} %get-tuple-element.2), channel_id=1, replica_groups=mesh['ep'=32,'tp'=8] {'tp'}, use_global_device_ids=true, to_apply=%region_9.10 | all-reduce | flops 256 | bytes 2048 | tf_op jit(solution)/shard_map/psum | solution.py:113
  600.6 0.8 fusion.49
  (19 shorter events, 0.3 us)
Async XLA Ops:
  7.2 348.5 %copy-start = (bf16[1,352,2048]{2,1,0:T(8,128)(2,1)S(1)}, bf16[1,352,2048]{2,1,0:T(8,128)(2,1)}, u32[]{:S(2)}) copy-start(bf16[1,352,2048]{2,1,0:T(8,128)(2,1)} %param.18) | copy-start | bytes 4325380
  7.2 3.2 copy-start.4
  7.2 76.2 %all-reduce.2.cloned.1.call-start = ((), (), s32[]{:S(2)}) async-start(), calls=%async_computation.3 | async-start | bytes 4194304 | tf_op jit(solution)/shard_map/psum | solution.py:50
  83.4 2.3 copy-start.5
  106.9 241.7 %all-to-all-start = ((bf16[32,2,40,2048]{3,2,1,0:T(8,128)(2,1)}), bf16[32,2,40,2048]{3,2,1,0:T(8,128)(2,1)}, u32[]{:S(2)}, u32[]{:S(2)}) async-start(bf16[32,2,40,2048]{3,2,1,0:T(8,128)(2,1)} %broadcast_select_fusion), calls=%async_computation | async-start | bytes 20971520 | tf_op jit(solution)/shard_map/all_to_all | solution.py:75
  365.5 11.1 %copy-start.3 = (bf16[2048,64]{0,1:T(8,128)(2,1)S(1)}, bf16[2048,64]{0,1:T(8,128)(2,1)}, u32[]{:S(2)}) copy-start(bf16[2048,64]{0,1:T(8,128)(2,1)} %param.16) | copy-start | bytes 786436
  365.5 127.3 %all-to-all-start.1 = ((bf16[32,40,2048]{2,1,0:T(8,128)(2,1)}), bf16[32,40,2048]{2,1,0:T(8,128)(2,1)}, u32[]{:S(2)}, u32[]{:S(2)}) async-start(bf16[32,40,2048]{2,1,0:T(8,128)(2,1)} %convolution_convert_fusion), calls=%async_computation.1 | async-start | bytes 10485760 | tf_op jit(solution)/shard_map/all_to_all | solution.py:90
  375.7 209.0 %reduce-scatter.2.cloned.1.call-start = ((), (), s32[]{:S(2)}) async-start(), calls=%async_computation.4 | async-start | bytes 1179648 | tf_op jit(solution)/shard_map/reduce_scatter | solution.py:107
  526.7 74.7 %copy-start.1 = (bf16[1,352,2048]{2,1,0:T(8,128)(2,1)S(1)}, bf16[1,352,2048]{2,1,0:T(8,128)(2,1)}, u32[]{:S(2)}) copy-start(bf16[1,352,2048]{2,1,0:T(8,128)(2,1)} %param.18) | copy-start | bytes 4325380
  585.7 15.7 %copy-start.2 = (bf16[256,256]{1,0:T(8,128)(2,1)}, bf16[256,256]{1,0:T(8,128)(2,1)S(1)}, u32[]{:S(2)}) copy-start(bf16[256,256]{1,0:T(8,128)(2,1)S(1)} %get-tuple-element.3) | copy-start | bytes 393220
Sparse Core Ops, SparseCore 0:
  10.5 72.8 all-reduce.1
  532.7 51.9 reduce-scatter.1
where the time goes:
time: 609 us; the launch traced here: 608 us
  waiting for transfers between devices  427 us (70%)
  local copies, waits for them, and re-layouts  60.9 us (10%)
  matrix products  36.1 us (6%)
  other arithmetic  33.8 us (6%)
  starting transfers between devices  20.1 us (3%)
  between operations  15 us (2%)
  blocking collectives  14.9 us (2%)
    all_to_all x1, waiting for transfers between devices, on_device(): lax.all_to_all(dispatched, 'ep', split_axis=0, concat_axis=0, tiled=True)  232 us
    all_to_all x1, waiting for transfers between devices, on_device(): lax.all_to_all(produced, 'ep', split_axis=0, concat_axis=0, tiled=True)  99.9 us
    reduce_scatter x1, waiting for transfers between devices, on_device(): lax.psum_scatter((routed_part + shared_part).astype(jnp.bfloat16), 'tp',...  51.3 us
    psum x1, waiting for transfers between devices, on_device(): summed = lax.psum(partial_out, 'tp')  44.1 us
    gather x2, local copies, waits for them, and re-layouts, on_device(): picked = flat_terms[term_row]  26.8 us
    another operation x3, other arithmetic  18.4 us
    psum x1, blocking collectives, on_device(): squares = lax.psum(jnp.sum(next_wide * next_wide, axis=1), 'tp')  14.9 us
    gather x5, local copies, waits for them, and re-layouts, gate_weights(): chosen = jnp.take_along_axis(logits, route_block, axis=1)  13.2 us
  transfers between devices with their start and end apart: 4, of which 4 were waited for; matrix products, arithmetic and copies ran while one was open for 8% of the time, Pallas kernels for 0%

commit v1 on v0

--- a/solution.py
+++ b/solution.py
@@ -47,7 +47,9 @@
     next_gain,
 ):
     partial_out = jnp.dot(attn_out, out_proj, preferred_element_type=jnp.float32)
-    summed = lax.psum(partial_out, "tp")
+    summed = partial_out
+    for hop in (1, 2, 4):
+        summed = summed + lax.ppermute(summed, "tp", [(dev, dev ^ hop) for dev in range(8)])
     stream = (summed + residual.astype(jnp.float32)).astype(jnp.bfloat16)
     stream_wide = stream.astype(jnp.float32)
     normed = (

time: 609 us -> 659 us (1.082)
  other arithmetic: 33.8 us -> 60.8 us
  local copies, waits for them, and re-layouts: 60.9 us -> 78.6 us
  starting transfers between devices: 20.1 us -> 33.4 us
  waiting for transfers between devices: 427 us -> 419 us
    ppermute x0 -> x3, waiting for transfers between devices: none -> 50.6 us  [on_device(): lax.ppermute(summed, 'tp', [(dev, dev ^ hop) for dev in range(8)])]
    psum x1 -> x0, waiting for transfers between devices: 44.1 us -> none  [on_device(): summed = lax.psum(partial_out, 'tp')]
    reduce_scatter x1, waiting for transfers between devices: 51.3 us -> 31.3 us  [on_device(): lax.psum_scatter((routed_part + shared_part).astype(jnp.bfloat16), 'tp',...]
    another operation x3, other arithmetic: 18.4 us -> 36.4 us
    all_to_all x1, starting transfers between devices: 10.2 us -> 17.1 us  [on_device(): lax.all_to_all(produced, 'ep', split_axis=0, concat_axis=0, tiled=True)]
  transfers between devices with their start and end apart: 4 -> 6, of which waited for: 4 -> 5; matrix products, arithmetic and copies ran while one was open for 8% -> 13% of each run, Pallas kernels for 0% -> 0%
where the time goes in v1:
time: 659 us; the launch traced here: 655 us
  waiting for transfers between devices  419 us (64%)
  local copies, waits for them, and re-layouts  78.6 us (12%)
  other arithmetic  60.8 us (9%)
  matrix products  34 us (5%)
  starting transfers between devices  33.4 us (5%)
  between operations  15 us (2%)
  blocking collectives  14.9 us (2%)
    all_to_all x1, waiting for transfers between devices, on_device(): lax.all_to_all(dispatched, 'ep', split_axis=0, concat_axis=0, tiled=True)  238 us
    all_to_all x1, waiting for transfers between devices, on_device(): lax.all_to_all(produced, 'ep', split_axis=0, concat_axis=0, tiled=True)  99 us
    ppermute x3, waiting for transfers between devices, on_device(): lax.ppermute(summed, 'tp', [(dev, dev ^ hop) for dev in range(8)])  50.6 us
    another operation x3, other arithmetic  36.4 us
    reduce_scatter x1, waiting for transfers between devices, on_device(): lax.psum_scatter((routed_part + shared_part).astype(jnp.bfloat16), 'tp',...  31.3 us
    gather x2, local copies, waits for them, and re-layouts, on_device(): picked = flat_terms[term_row]  26.8 us
    all_to_all x1, starting transfers between devices, on_device(): lax.all_to_all(produced, 'ep', split_axis=0, concat_axis=0, tiled=True)  17.1 us
    psum x1, blocking collectives, on_device(): squares = lax.psum(jnp.sum(next_wide * next_wide, axis=1), 'tp')  14.9 us
  transfers between devices with their start and end apart: 6, of which 5 were waited for; matrix products, arithmetic and copies ran while one was open for 13% of the time, Pallas kernels for 0%

profile of v1, /device:TPU:1, one launch (start us, length us, event | category | flops | bytes accessed | tf_op | source)
XLA Modules:
  0.0 655.4 jit_solution(11748817112359304546)
XLA Ops:
  7.2 1.8 fusion.67
  9.0 3.3 collective-permute-start
  12.3 3.8 collective-permute-done
  16.1 0.3 add.146
  16.6 46.8 %collective-permute-done.1 = f32[256,2048]{1,0:T(8,128)S(1)} collective-permute-done((f32[256,2048]{1,0:T(8,128)S(1)}, f32[256,2048]{1,0:T(8,128)S(1)}, u32[]{:S(2)}, u32[]{:S(2)}) %collective-permute-start.1) | collective-permute-done | bytes 2097184 | tf_op jit(solution)/shard_map/ppermute | solution.py:52
  63.4 0.3 add.147
  63.7 1.3 collective-permute-start.2
  65.0 0.8 copy.42
  65.8 1.0 eq.37
  66.8 1.6 eq.33
  69.1 0.9 fusion.29
  70.0 34.5 %reduce-window.6 = s32[64,12,128]{2,1,0:T(8,128)} reduce-window(s32[64,12,128]{2,1,0:T(8,128)} %fusion.29, s32[]{:T(128)} %constant.103.clone.1), window={size=1x1x128 pad=0_0x0_0x127_0}, to_apply=%region_0.0 | reduce-window | flops 12484608 | bytes 786436 | tf_op jit(solution)/shard_map/reduce-window
  104.5 2.1 slice.30
  106.5 1.3 copy.44
  107.8 0.6 reduce-window.9
  108.4 1.4 copy.45
  109.9 1.2 broadcast_add_fusion
  111.1 0.9 fusion.32
  112.0 0.8 reduce_sum.43
  112.8 1.6 copy.46
  114.4 1.3 compare_select_fusion.3
  115.7 1.5 copy.41
  117.2 1.6 mul.91
  118.8 1.3 fusion.58
  120.1 6.9 %scatter_custom_fusion = s32[2560]{0:T(1024)} fusion(s32[1536]{0:T(1024)} %fusion.58, s32[1536]{0:T(1024)S(1)} %iota.72, s32[]{:T(128)} %constant.107.clone.1), kind=kCustom, calls=%fused_computation.106 | custom fusion | bytes 10752 | tf_op jit(solution)/shard_map/scatter | solution.py:23
  127.0 0.7 fusion.43
  127.7 0.7 ge.28
  128.5 0.7 ge.27
  129.2 1.3 broadcast_divide_fusion
  130.5 1.4 div.89
  131.9 0.7 and.83
  132.6 1.5 compare_select_fusion
  134.1 1.5 reshape.223
  135.5 1.3 pad_clamp_fusion
  136.8 2.4 fusion.7
  139.3 0.9 copy-done.2
  140.3 0.3 fusion.9
  140.6 10.8 %gather_fusion = bf16[2560,2048]{1,0:T(8,128)(2,1)} fusion(bf16[256,2048]{1,0:T(8,128)(2,1)S(1)} %fusion.9, s32[3072]{0:T(1024)S(1)} %copy-done.6), kind=kCustom, calls=%fused_computation | custom fusion | bytes 20981760 | tf_op jit(solution)/shard_map/gather | solution.py:75
  151.4 10.0 %broadcast_select_fusion = bf16[32,2,40,2048]{3,2,1,0:T(8,128)(2,1)} fusion(bf16[32,2,40,2048]{3,2,1,0:T(8,128)(2,1)} %bitcast.81, pred[32,2,40]{2,1,0:T(4,128)(4,1)S(1)} %copy-done.7), kind=kLoop, calls=%fused_computation.4 | loop fusion | flops 5242880 | bytes 20974080 | tf_op jit(solution)/shard_map/jit(_where)/select_n | solution.py:75
  161.3 11.3 %all-to-all-start = ((bf16[32,2,40,2048]{3,2,1,0:T(8,128)(2,1)}), bf16[32,2,40,2048]{3,2,1,0:T(8,128)(2,1)}, u32[]{:S(2)}, u32[]{:S(2)}) async-start(bf16[32,2,40,2048]{3,2,1,0:T(8,128)(2,1)} %broadcast_select_fusion), calls=%async_computation | async-start | bytes 20971520 | tf_op jit(solution)/shard_map/all_to_all | solution.py:77
  172.7 237.8 %all-to-all-done = bf16[32,2,40,2048]{3,2,1,0:T(8,128)(2,1)} async-done(((bf16[32,2,40,2048]{3,2,1,0:T(8,128)(2,1)}), bf16[32,2,40,2048]{3,2,1,0:T(8,128)(2,1)}, u32[]{:S(2)}, u32[]{:S(2)}) %all-to-all-start) | async-done | bytes 10485792 | tf_op jit(solution)/shard_map/all_to_all | solution.py:77
  410.4 7.1 %fusion.2 = f32[32,40,352]{2,1,0:T(8,128)} fusion(bf16[32,2,40,2048]{3,2,1,0:T(8,128)(2,1)} %all-to-all-done, s32[]{:T(128)S(6)} %select_n.135, bf16[1,2,352,2048]{3,2,1,0:T(8,128)(2,1)} %param.17), kind=kOutput, calls=%fused_computation.7 | convolution fusion | flops 1845493760 | bytes 8486916 | tf_op jit(solution)/shard_map/scd,fd->scf/dot_general | solution.py:82
  417.6 9.8 %convolution_convert_fusion = bf16[32,40,2048]{2,1,0:T(8,128)(2,1)} fusion(bf16[1,352,2048]{2,1,0:T(8,128)(2,1)S(1)} %copy-done, f32[32,40,352]{2,1,0:T(8,128)} %fusion.2, bf16[32,2,40,2048]{3,2,1,0:T(8,128)(2,1)} %all-to-all-done, s32[]{:T(128)S(6)} %select_n.135, bf16[1,2,352,2048]{3,2,1,0:T(8,128)(2,1)} %param.17), kind=kOutput, calls=%fused_computation.11 | convolution fusion | flops 3696312320 | bytes 15335428 | tf_op jit(solution)/shard_map/scf,fd->scd/dot_general | solution.py:89
  427.3 17.1 %all-to-all-start.1 = ((bf16[32,40,2048]{2,1,0:T(8,128)(2,1)}), bf16[32,40,2048]{2,1,0:T(8,128)(2,1)}, u32[]{:S(2)}, u32[]{:S(2)}) async-start(bf16[32,40,2048]{2,1,0:T(8,128)(2,1)} %convolution_convert_fusion), calls=%async_computation.1 | async-start | bytes 10485760 | tf_op jit(solution)/shard_map/all_to_all | solution.py:92
  444.4 0.3 reduce-scatter.2.cloned.1.call-start
  444.7 0.1 copy.47
  444.9 0.1 reshape.231
  445.0 0.1 copy.48
  445.2 0.1 reshape.237
  445.3 0.4 fusion.68
  445.8 12.7 %gather_fusion.2 = f32[1536]{0:T(1024)S(1)} fusion(f32[256,64]{0,1:T(8,128)S(1)} %fusion.68, s32[1536]{0:T(1024)S(1)} %reshape.237), kind=kCustom, calls=%fused_computation.2 | custom fusion | bytes 24576 | tf_op jit(solution)/shard_map/jit(take_along_axis)/gather | solution.py:30
  458.5 0.1 reshape.240
  458.8 0.2 copy.50
  459.0 1.9 fusion.14
  460.9 99.0 %all-to-all-done.1 = bf16[32,40,2048]{2,1,0:T(8,128)(2,1)} async-done(((bf16[32,40,2048]{2,1,0:T(8,128)(2,1)}), bf16[32,40,2048]{2,1,0:T(8,128)(2,1)}, u32[]{:S(2)}, u32[]{:S(2)}) %all-to-all-start.1) | async-done | bytes 5242912 | tf_op jit(solution)/shard_map/all_to_all | solution.py:92
  559.9 15.8 %gather_fusion.1 = bf16[1536,2048]{1,0:T(8,128)(2,1)} fusion(bf16[1280,2048]{1,0:T(8,128)(2,1)} %bitcast.11, s32[2048]{0:T(1024)S(1)} %pad_clamp_fusion.1), kind=kCustom, calls=%fused_computation.1 | custom fusion | bytes 12589056 | tf_op jit(solution)/shard_map/gather | solution.py:99
  575.8 10.9 %reshape.230 = bf16[256,6,2048]{2,1,0:T(8,128)(2,1)} reshape(bf16[1536,2048]{1,0:T(8,128)(2,1)} %gather_fusion.1) | data formatting | bytes 12582912 | tf_op jit(solution)/shard_map/gather | solution.py:99
  586.7 7.1 %fusion.69 = f32[256,1,2048]{2,1,0:T(1,128)} fusion(bf16[256,6,2048]{2,1,0:T(8,128)(2,1)} %reshape.230, bf16[256,6,1]{1,2,0:T(2,128)(2,1)S(1)} %copy.50), kind=kOutput, calls=%fused_computation.118 | convolution fusion | flops 6291456 | bytes 8391680 | tf_op jit(solution)/shard_map/tkd,tk->td/dot_general | solution.py:100
  593.8 5.8 fusion.6
  599.6 0.8 dynamic_slice.12
  600.4 31.3 %reduce-scatter.2.cloned.1.call-done = bf16[256,256]{1,0:T(8,128)(2,1)} async-done(((bf16[256,2048]{1,0:T(8,128)(2,1)}), bf16[256,256]{1,0:T(8,128)(2,1)}) %reduce-scatter.2.cloned.1.call-update) | async-done | bytes 131088 | tf_op jit(solution)/shard_map/reduce_scatter | solution.py:109
  631.7 1.1 fusion.34
  632.8 14.9 %psum.7 = f32[256]{0:T(256)S(1)} all-reduce(f32[256]{0:T(256)S(1)} %get-tuple-element.2), channel_id=1, replica_groups=mesh['ep'=32,'tp'=8] {'tp'}, use_global_device_ids=true, to_apply=%region_8.9 | all-reduce | flops 256 | bytes 2048 | tf_op jit(solution)/shard_map/psum | solution.py:115
  647.7 0.8 fusion.36
  (32 shorter events, 0.4 us)
Async XLA Ops:
  7.2 410.4 %copy-start = (bf16[1,352,2048]{2,1,0:T(8,128)(2,1)S(1)}, bf16[1,352,2048]{2,1,0:T(8,128)(2,1)}, u32[]{:S(2)}) copy-start(bf16[1,352,2048]{2,1,0:T(8,128)(2,1)} %param.18) | copy-start | bytes 4325380
  9.0 7.1 %collective-permute-start = (f32[256,2048]{1,0:T(8,128)S(1)}, f32[256,2048]{1,0:T(8,128)S(1)}, u32[]{:S(2)}, u32[]{:S(2)}) collective-permute-start(f32[256,2048]{1,0:T(8,128)S(1)} %fusion.67), channel_id=1, source_target_pairs={{0,1},{1,0},{2,3},{3,2},{4,5},{5,4},{6,7},{7,6},{8,9},{9,8},{10,11... | collective-permute-start | bytes 6291464 | tf_op jit(solution)/shard_map/ppermute | solution.py:52
  16.5 48.5 %copy-start.5 = (s32[256,6]{0,1:T(8,128)S(1)}, s32[256,6]{0,1:T(8,128)}, u32[]{:S(2)}) copy-start(s32[256,6]{0,1:T(8,128)} %param.21) | copy-start | bytes 18436
  16.5 46.9 %collective-permute-start.1 = (f32[256,2048]{1,0:T(8,128)S(1)}, f32[256,2048]{1,0:T(8,128)S(1)}, u32[]{:S(2)}, u32[]{:S(2)}) collective-permute-start(f32[256,2048]{1,0:T(8,128)S(1)} %add.146), channel_id=1, source_target_pairs={{0,2},{1,3},{2,0},{3,1},{4,6},{5,7},{6,4},{7,5},{8,10},{9,11},{10,... | collective-permute-start | bytes 6291464 | tf_op jit(solution)/shard_map/ppermute | solution.py:52
  63.7 73.1 %collective-permute-start.2 = (f32[256,2048]{1,0:T(8,128)S(1)}, f32[256,2048]{1,0:T(8,128)}, u32[]{:S(2)}, u32[]{:S(2)}) collective-permute-start(f32[256,2048]{1,0:T(8,128)S(1)} %add.147), channel_id=1, source_target_pairs={{0,4},{1,5},{2,6},{3,7},{4,0},{5,1},{6,2},{7,3},{8,12},{9,13},{10,... | collective-permute-start | bytes 6291464 | tf_op jit(solution)/shard_map/ppermute | solution.py:52
  136.8 3.4 copy-start.9
  139.3 1.0 copy-start.2
  139.3 1.3 copy-start.6
  140.6 10.8 %copy-start.7 = (pred[32,2,40]{2,1,0:T(4,128)(4,1)S(1)}, pred[32,2,40]{2,1,0:T(4,128)(4,1)}, u32[]{:S(2)}) copy-start(pred[32,2,40]{2,1,0:T(4,128)(4,1)} %ge.27) | copy-start | bytes 7684
  161.3 249.1 %all-to-all-start = ((bf16[32,2,40,2048]{3,2,1,0:T(8,128)(2,1)}), bf16[32,2,40,2048]{3,2,1,0:T(8,128)(2,1)}, u32[]{:S(2)}, u32[]{:S(2)}) async-start(bf16[32,2,40,2048]{3,2,1,0:T(8,128)(2,1)} %broadcast_select_fusion), calls=%async_computation | async-start | bytes 20971520 | tf_op jit(solution)/shard_map/all_to_all | solution.py:77
  427.3 17.4 %copy-start.8 = (s32[256,6]{0,1:T(8,128)S(1)}, s32[256,6]{0,1:T(8,128)}, u32[]{:S(2)}) copy-start(s32[256,6]{0,1:T(8,128)} %get-tuple-element.8) | copy-start | bytes 18436
  427.3 18.0 %copy-start.4 = (bf16[2048,64]{0,1:T(8,128)(2,1)S(1)}, bf16[2048,64]{0,1:T(8,128)(2,1)}, u32[]{:S(2)}) copy-start(bf16[2048,64]{0,1:T(8,128)(2,1)} %param.16) | copy-start | bytes 786436
  427.3 132.6 %all-to-all-start.1 = ((bf16[32,40,2048]{2,1,0:T(8,128)(2,1)}), bf16[32,40,2048]{2,1,0:T(8,128)(2,1)}, u32[]{:S(2)}, u32[]{:S(2)}) async-start(bf16[32,40,2048]{2,1,0:T(8,128)(2,1)} %convolution_convert_fusion), calls=%async_computation.1 | async-start | bytes 10485760 | tf_op jit(solution)/shard_map/all_to_all | solution.py:92
  444.4 187.3 %reduce-scatter.2.cloned.1.call-start = ((), (), s32[]{:S(2)}) async-start(), calls=%async_computation.3 | async-start | bytes 1179648 | tf_op jit(solution)/shard_map/reduce_scatter | solution.py:109
  593.8 54.7 %copy-start.1 = (bf16[1,352,2048]{2,1,0:T(8,128)(2,1)S(1)}, bf16[1,352,2048]{2,1,0:T(8,128)(2,1)}, u32[]{:S(2)}) copy-start(bf16[1,352,2048]{2,1,0:T(8,128)(2,1)} %param.18) | copy-start | bytes 4325380
  632.8 15.7 %copy-start.3 = (bf16[256,256]{1,0:T(8,128)(2,1)}, bf16[256,256]{1,0:T(8,128)(2,1)S(1)}, u32[]{:S(2)}) copy-start(bf16[256,256]{1,0:T(8,128)(2,1)S(1)} %get-tuple-element.3) | copy-start | bytes 393220
Sparse Core Ops, SparseCore 0:
  599.8 31.9 reduce-scatter.1
